TPU v7x, 32 devices: a whole 2x2x4 slice. The times are simulated.
32 devices in a mesh: prow: 8 (over z, y), pcol: 4 (over x, core).
Axes of the slice: x: 2, y: 2, z: 4, core: 2. Of those that a mesh axis runs over, the one named last changes fastest.
Arguments:
- paper_x: bfloat16 [8192, 768], P(('prow', 'pcol')), may hold values from -6 to 6
- author_x: bfloat16 [4096, 768], P(('pcol', 'prow')), may hold values from -6 to 6
- w_self: bfloat16 [768, 768], replicated, may hold values from -0.21875 to 0.21875
- w_rel: bfloat16 [2, 768, 768], replicated, may hold values from -0.009765625 to 0.009765625
- w_two: bfloat16 [768, 768], replicated, may hold values from -0.0068359375 to 0.0068359375
- block_rows: int32 [8, 4, 32], P('prow', 'pcol'), may hold values from 0 to 7, as said below
- block_cols: int32 [8, 4, 32], P('prow', 'pcol'), may hold values from 0 to 7, as said below
- block_type: int32 [8, 4, 32], P('prow', 'pcol'), may hold values from 0 to 1
- block_count: int32 [8, 4], P('prow', 'pcol'), may hold values from 8 to 32, as said below
- block_vals: bfloat16 [8, 4, 32, 128, 128], P('prow', 'pcol'), may hold values from 0 to 1, as said below
Outputs:
- paper_hidden: bfloat16 [8192, 768], P(('prow', 'pcol'))
- author_out: bfloat16 [4096, 768], P(('pcol', 'prow'))
Inputs may be any that keep to these rules, and one draw needn't show every extreme that they name: `block_rows`: within one tile the live and dead slots name distinct positions; block rows are below 8. `block_cols`: block columns are below 8; with block_rows, positions of one tile are distinct. `block_count`: slots 0 to count - 1 of a tile are live; some tile holds 32 live slots and some tile 32 // 4 in every draw. `block_vals`: every entry is 0 or 1.
All inputs are finite; a program needn't handle non-finite values.
Results may differ from a plain program's by a relative error of at most 0.0041.
Values may be sent and summed in bfloat16 or wider, within the bound.
A program may use at most 64 MiB of HBM per device.

v0:
```python
import jax
import jax.numpy as jnp
from jax import lax
from jax.sharding import PartitionSpec as P

GROUP = 16


def per_device(
    paper_x,
    author_x,
    w_self,
    w_rel,
    w_two,
    block_rows,
    block_cols,
    block_type,
    block_count,
    block_vals,
):
    slots = block_rows.shape[2]
    side = block_vals.shape[3]
    width = paper_x.shape[1]
    relations = w_rel.shape[0]
    groups = slots // GROUP
    own_rows = paper_x.shape[0]
    row_ids = block_rows.reshape(groups, GROUP)
    col_ids = block_cols.reshape(groups, GROUP)
    type_ids = block_type.reshape(groups, GROUP)
    live = (
        (jnp.arange(slots, dtype=jnp.int32) < block_count.reshape(()))
        .astype(jnp.float32)
        .reshape(groups, GROUP)
    )
    contents = block_vals.reshape(groups, GROUP, side, side)
    self_term = jnp.dot(paper_x, w_self, preferred_element_type=jnp.float32)
    authors = lax.all_gather(author_x, "prow", axis=0, tiled=True)
    messages = jnp.stack(
        [
            jnp.dot(authors, w_rel[index], preferred_element_type=jnp.float32)
            for index in range(relations)
        ]
    ).astype(jnp.bfloat16)
    col_blocks = messages.shape[1] // side
    row_blocks = own_rows * lax.axis_size("pcol") // side
    table = messages.reshape(relations * col_blocks, side, width)
    row_range = jnp.arange(row_blocks, dtype=jnp.int32)
    col_range = jnp.arange(col_blocks, dtype=jnp.int32)

    def first_hop(total, item):
        rows_now, cols_now, types_now, mask_now, content_now = item
        picked = table[types_now * col_blocks + cols_now]
        product = jnp.einsum(
            "kpa,kaf->kpf", content_now, picked, preferred_element_type=jnp.float32
        )
        placing = (rows_now[:, None] == row_range[None, :]).astype(jnp.float32) * mask_now[:, None]
        return (
            total + jnp.einsum("kr,kpf->rpf", placing, product, precision=lax.Precision.HIGHEST),
            None,
        )

    start = jnp.zeros((row_blocks, side, width), jnp.float32)
    partial_value, _ = lax.scan(first_hop, start, (row_ids, col_ids, type_ids, live, contents))
    partial_value = partial_value.reshape(row_blocks * side, width)
    summed = lax.psum_scatter(partial_value, "pcol", scatter_dimension=0, tiled=True)
    paper_hidden = jnp.maximum(self_term + summed, 0.0).astype(jnp.bfloat16)
    outgoing = jnp.dot(paper_hidden, w_two, preferred_element_type=jnp.float32).astype(jnp.bfloat16)
    paper_rows = lax.all_gather(outgoing, "pcol", axis=0, tiled=True).reshape(
        row_blocks, side, width
    )

    def second_hop(total, item):
        rows_now, cols_now, mask_now, content_now = item
        picked = paper_rows[rows_now]
        product = jnp.einsum(
            "kpa,kpf->kaf", content_now, picked, preferred_element_type=jnp.float32
        )
        placing = (cols_now[:, None] == col_range[None, :]).astype(jnp.float32) * mask_now[:, None]
        return (
            total + jnp.einsum("kc,kaf->caf", placing, product, precision=lax.Precision.HIGHEST),
            None,
        )

    start_two = jnp.zeros((col_blocks, side, width), jnp.float32)
    author_part, _ = lax.scan(second_hop, start_two, (row_ids, col_ids, live, contents))
    author_total = lax.psum_scatter(
        author_part.reshape(col_blocks * side, width), "prow", scatter_dimension=0, tiled=True
    )
    return (paper_hidden, author_total.astype(jnp.bfloat16))


def solution(mesh):
    return jax.shard_map(
        per_device,
        mesh=mesh,
        in_specs=(
            P(("prow", "pcol"), None),
            P(("pcol", "prow"), None),
            P(),
            P(),
            P(),
            P("prow", "pcol", None),
            P("prow", "pcol", None),
            P("prow", "pcol", None),
            P("prow", "pcol"),
            P("prow", "pcol", None, None, None),
        ),
        out_specs=(P(("prow", "pcol"), None), P(("pcol", "prow"), None)),
        check_vma=False,
    )
```

profile of v0, /device:TPU:0, one launch (start us, length us, event | category | flops | bytes accessed | tf_op | source)
XLA Modules:
  0.0 299.5 jit_solution(3397042512454895330)
XLA Ops:
  7.2 0.7 all-gather.3.cloned.1.call-update
  8.0 0.5 broadcast.116
  8.5 1.3 reduce.9
  9.9 1.3 reduce.11
  11.3 1.3 reduce.10
  13.4 43.8 %all-gather.3.cloned.1.call-done = bf16[1024,768]{1,0:T(8,128)(2,1)} async-done(((bf16[128,768]{1,0:T(8,128)(2,1)}), bf16[1024,768]{1,0:T(8,128)(2,1)}) %all-gather.3.cloned.1.call-update) | async-done | bytes 1572880 | tf_op jit(solution)/shard_map/all_gather | solution.py:37
  57.1 3.3 %fusion.41 = bf16[1,1024,768]{2,1,0:T(8,128)(2,1)S(1)} fusion(bf16[1024,768]{1,0:T(8,128)(2,1)} %all-gather.3.cloned.1.call-done, bf16[2,768,768]{2,1,0:T(8,128)(2,1)} %param.17), kind=kOutput, calls=%fused_computation.55 | convolution fusion | flops 1208745984 | bytes 4325376 | tf_op jit(solution)/shard_map/dot_general | solution.py:40
  60.4 1.4 fusion.42
  61.8 2.0 pad_maximum_fusion
  63.8 41.9 %while.22 = (s32[]{:T(128)}, f32[8,128,768]{2,0,1:T(8,128)}, s32[2,16]{1,0:T(2,128)S(1)}, f32[2,16]{1,0:T(2,128)S(1)}, bf16[2,16,128,128]{3,2,1,0:T(8,128)(2,1)S...) while((s32[]{:T(128)}, f32[8,128,768]{2,0,1:T(8,128)}, ...), condition=%wide.region_1.2_spmd.clone, body=%wide.region_0.1_spmd.clone.sunk | while | flops 555222400 | bytes 28840768 | solution.py:63
  63.8 4.3 %gather_fusion = bf16[16,128,768]{2,1,0:T(8,128)(2,1)} fusion(bf16[16,128,768]{2,1,0:T(8,128)(2,1)} %get-tuple-element.297, s32[1024]{0:T(1024)S(1)} %pad_clamp_fusion.4), kind=kCustom, calls=%fused_computation.clone.clone.1 | custom fusion | bytes 6291520 | tf_op jit(solution)/shard_map/while/body/eval_jaxpr/gather | solution.py:52
  68.1 5.5 %fusion.78 = f32[16,128,768]{2,1,0:T(8,128)} fusion(bf16[16,128,768]{2,1,0:T(8,128)(2,1)} %gather_fusion, bf16[2,16,128,128]{3,2,1,0:T(8,128)(2,1)S(1)} %get-tuple-element.294, s32[]{:T(128)} %get-tuple-element.280), kind=kOutput, calls=%fused_computation.7.clone.1 | convolution fusion | flops 402653184 | bytes 9961476 | tf_op jit(solution)/shard_map/while/body/eval_jaxpr/kpa,kaf->kpf/dot_general | solution.py:53
  73.6 10.9 %select_add_fusion.4 = f32[8,128,768]{2,0,1:T(8,128)} fusion(f32[8,128,768]{2,0,1:T(8,128)} %get-tuple-element.281, f32[16,128,768]{2,1,0:T(8,128)} %fusion.78, pred[]{:T(512)S(6)} %compare.6, f32[16]{0:T(128)S(1)} %fusion.79, s32[16]{0:T(128)S(1)} %fusion.80), kind=kOutput, calls=%fused_computation.6.clone.1 | convolution fusion | flops 152568064 | bytes 12583041 | tf_op jit(solution)/shard_map/while/body/eval_jaxpr/kr,kpf->rpf/dot_general | solution.py:58
  84.5 4.3 %gather_fusion = bf16[16,128,768]{2,1,0:T(8,128)(2,1)} fusion(bf16[16,128,768]{2,1,0:T(8,128)(2,1)} %get-tuple-element.297, s32[1024]{0:T(1024)S(1)} %pad_clamp_fusion.4), kind=kCustom, calls=%fused_computation.clone.clone.1 | custom fusion | bytes 6291520 | tf_op jit(solution)/shard_map/while/body/eval_jaxpr/gather | solution.py:52
  88.8 5.5 %fusion.78 = f32[16,128,768]{2,1,0:T(8,128)} fusion(bf16[16,128,768]{2,1,0:T(8,128)(2,1)} %gather_fusion, bf16[2,16,128,128]{3,2,1,0:T(8,128)(2,1)S(1)} %get-tuple-element.294, s32[]{:T(128)} %get-tuple-element.280), kind=kOutput, calls=%fused_computation.7.clone.1 | convolution fusion | flops 402653184 | bytes 9961476 | tf_op jit(solution)/shard_map/while/body/eval_jaxpr/kpa,kaf->kpf/dot_general | solution.py:53
  94.3 11.4 %select_add_fusion.4 = f32[8,128,768]{2,0,1:T(8,128)} fusion(f32[8,128,768]{2,0,1:T(8,128)} %get-tuple-element.281, f32[16,128,768]{2,1,0:T(8,128)} %fusion.78, pred[]{:T(512)S(6)} %compare.6, f32[16]{0:T(128)S(1)} %fusion.79, s32[16]{0:T(128)S(1)} %fusion.80), kind=kOutput, calls=%fused_computation.6.clone.1 | convolution fusion | flops 152568064 | bytes 12583041 | tf_op jit(solution)/shard_map/while/body/eval_jaxpr/kr,kpf->rpf/dot_general | solution.py:58
  105.7 4.6 %copy.12 = f32[8,128,768]{2,1,0:T(8,128)} copy(f32[8,128,768]{2,0,1:T(8,128)} %get-tuple-element.91) | data formatting | bytes 6291456 | tf_op jit(solution)/shard_map/while | solution.py:63
  110.3 36.3 %reduce-scatter.3.cloned.1.call-done = f32[256,768]{1,0:T(8,128)} async-done(((f32[1024,768]{1,0:T(8,128)}), f32[256,768]{1,0:T(8,128)}) %reduce-scatter.3.cloned.1.call-update) | async-done | bytes 786448 | tf_op jit(solution)/shard_map/reduce_scatter | solution.py:65
  146.7 1.6 fusion.44
  148.3 2.6 convolution_convert_fusion.2
  151.0 0.2 reduce-scatter.5.cloned.1.call-start
  151.2 19.5 %all-gather.5.cloned.1.call-done = bf16[1024,768]{1,0:T(8,128)(2,1)} async-done(((bf16[256,768]{1,0:T(8,128)(2,1)}), bf16[1024,768]{1,0:T(8,128)(2,1)}) %all-gather.5.cloned.1.call-update) | async-done | bytes 1572880 | tf_op jit(solution)/shard_map/all_gather | solution.py:68
  170.8 41.2 %while.23 = (s32[]{:T(128)}, f32[8,128,768]{2,0,1:T(8,128)}, s32[2,16]{1,0:T(2,128)S(1)}, f32[2,16]{1,0:T(2,128)S(1)}, bf16[2,16,128,128]{3,2,1,0:T(8,128)(2,1)S...) while((s32[]{:T(128)}, f32[8,128,768]{2,0,1:T(8,128)}, ...), condition=%wide.region_4.5_spmd.clone, body=%wide.region_3.4_spmd.clone.sunk | while | flops 555222336 | bytes 28840696 | solution.py:85
  170.8 3.8 %gather_fusion.1 = bf16[16,128,768]{2,1,0:T(8,128)(2,1)} fusion(bf16[8,128,768]{2,1,0:T(8,128)(2,1)} %get-tuple-element.324, s32[1024]{0:T(1024)S(1)} %pad_clamp_fusion.5), kind=kCustom, calls=%fused_computation.1.clone.clone.1 | custom fusion | bytes 6291520 | tf_op jit(solution)/shard_map/while/body/eval_jaxpr/gather | solution.py:74
  174.6 5.6 %fusion.86 = f32[16,128,768]{2,1,0:T(8,128)} fusion(bf16[16,128,768]{2,1,0:T(8,128)(2,1)} %gather_fusion.1, bf16[2,16,128,128]{3,2,1,0:T(8,128)(2,1)S(1)} %get-tuple-element.322, s32[]{:T(128)} %get-tuple-element.309), kind=kOutput, calls=%fused_computation.32.clone.1 | convolution fusion | flops 402653184 | bytes 9961476 | tf_op jit(solution)/shard_map/while/body/eval_jaxpr/kpa,kpf->kaf/dot_general | solution.py:75
  180.2 11.0 %select_add_fusion.5 = f32[8,128,768]{2,0,1:T(8,128)} fusion(f32[8,128,768]{2,0,1:T(8,128)} %get-tuple-element.310, f32[16,128,768]{2,1,0:T(8,128)} %fusion.86, pred[]{:T(512)S(6)} %compare.7, f32[16]{0:T(128)S(1)} %fusion.87, s32[16]{0:T(128)S(1)} %fusion.88), kind=kOutput, calls=%fused_computation.31.clone.1 | convolution fusion | flops 152568064 | bytes 12583041 | tf_op jit(solution)/shard_map/while/body/eval_jaxpr/kc,kaf->caf/dot_general | solution.py:80
  191.2 3.8 %gather_fusion.1 = bf16[16,128,768]{2,1,0:T(8,128)(2,1)} fusion(bf16[8,128,768]{2,1,0:T(8,128)(2,1)} %get-tuple-element.324, s32[1024]{0:T(1024)S(1)} %pad_clamp_fusion.5), kind=kCustom, calls=%fused_computation.1.clone.clone.1 | custom fusion | bytes 6291520 | tf_op jit(solution)/shard_map/while/body/eval_jaxpr/gather | solution.py:74
  195.0 5.6 %fusion.86 = f32[16,128,768]{2,1,0:T(8,128)} fusion(bf16[16,128,768]{2,1,0:T(8,128)(2,1)} %gather_fusion.1, bf16[2,16,128,128]{3,2,1,0:T(8,128)(2,1)S(1)} %get-tuple-element.322, s32[]{:T(128)} %get-tuple-element.309), kind=kOutput, calls=%fused_computation.32.clone.1 | convolution fusion | flops 402653184 | bytes 9961476 | tf_op jit(solution)/shard_map/while/body/eval_jaxpr/kpa,kpf->kaf/dot_general | solution.py:75
  200.5 11.4 %select_add_fusion.5 = f32[8,128,768]{2,0,1:T(8,128)} fusion(f32[8,128,768]{2,0,1:T(8,128)} %get-tuple-element.310, f32[16,128,768]{2,1,0:T(8,128)} %fusion.86, pred[]{:T(512)S(6)} %compare.7, f32[16]{0:T(128)S(1)} %fusion.87, s32[16]{0:T(128)S(1)} %fusion.88), kind=kOutput, calls=%fused_computation.31.clone.1 | convolution fusion | flops 152568064 | bytes 12583041 | tf_op jit(solution)/shard_map/while/body/eval_jaxpr/kc,kaf->caf/dot_general | solution.py:80
  212.0 4.6 %copy.13 = f32[8,128,768]{2,1,0:T(8,128)} copy(f32[8,128,768]{2,0,1:T(8,128)} %get-tuple-element.92) | data formatting | bytes 6291456 | tf_op jit(solution)/shard_map/while | solution.py:85
  216.5 74.7 %reduce-scatter.5.cloned.1.call-done = f32[128,768]{1,0:T(8,128)} async-done(((f32[1024,768]{1,0:T(8,128)}), f32[128,768]{1,0:T(8,128)}) %reduce-scatter.5.cloned.1.call-update) | async-done | bytes 393232 | tf_op jit(solution)/shard_map/reduce_scatter | solution.py:86
  291.2 1.7 convert_element_type.24
  (40 shorter events, 0.6 us)
Async XLA Ops:
  7.2 139.5 %copy-start = (bf16[768,768]{1,0:T(8,128)(2,1)S(1)}, bf16[768,768]{1,0:T(8,128)(2,1)}, u32[]{:S(2)}) copy-start(bf16[768,768]{1,0:T(8,128)(2,1)} %param.16) | copy-start | bytes 3538948
  7.2 49.9 %all-gather.3.cloned.1.call-start = ((), (), s32[]{:S(2)}) async-start(), calls=%async_computation.2 | async-start | bytes 1769472 | tf_op jit(solution)/shard_map/all_gather | solution.py:37
  7.9 138.8 %reduce-scatter.3.cloned.1.call-start = ((), (), s32[]{:S(2)}) async-start(), calls=%async_computation.3 | async-start | bytes 3932160 | tf_op jit(solution)/shard_map/reduce_scatter | solution.py:65
  57.1 3.3 %copy-start.4 = (bf16[2,768,768]{2,1,0:T(8,128)(2,1)S(1)}, bf16[2,768,768]{2,1,0:T(8,128)(2,1)}, u32[]{:S(2)}) copy-start(bf16[2,768,768]{2,1,0:T(8,128)(2,1)} %param.17) | copy-start | bytes 7077892
  57.1 3.3 %copy-start.5 = (bf16[1024,768]{1,0:T(8,128)(2,1)S(1)}, bf16[1024,768]{1,0:T(8,128)(2,1)}, u32[]{:S(2)}) copy-start(bf16[1024,768]{1,0:T(8,128)(2,1)} %all-gather.3.cloned.1.call-done) | copy-start | bytes 4718596
  61.8 2.0 copy-start.1
  110.3 36.4 %copy-start.3 = (bf16[256,768]{1,0:T(8,128)(2,1)S(1)}, bf16[256,768]{1,0:T(8,128)(2,1)}, u32[]{:S(2)}) copy-start(bf16[256,768]{1,0:T(8,128)(2,1)} %param.14) | copy-start | bytes 1179652
  110.3 60.5 %all-gather.5.cloned.1.call-start = ((), (), s32[]{:S(2)}) async-start(), calls=%async_computation.4 | async-start | bytes 1966080 | tf_op jit(solution)/shard_map/all_gather | solution.py:68
  148.3 22.5 %copy-start.2 = (bf16[256,768]{1,0:T(8,128)(2,1)}, bf16[256,768]{1,0:T(8,128)(2,1)S(1)}, u32[]{:S(2)}) copy-start(bf16[256,768]{1,0:T(8,128)(2,1)S(1)} %fusion.44) | copy-start | bytes 1179652
  151.0 140.3 %reduce-scatter.5.cloned.1.call-start = ((), (), s32[]{:S(2)}) async-start(), calls=%async_computation.5 | async-start | bytes 3538944 | tf_op jit(solution)/shard_map/reduce_scatter | solution.py:86
Sparse Core Ops, SparseCore 0:
  10.2 46.8 all-gather.2
  110.4 36.2 reduce-scatter.2
  151.1 19.6 all-gather.4
  216.7 74.5 reduce-scatter.4
where the time goes:
time: 300 us; the launch traced here: 299 us
  waiting for transfers between devices  175 us (58%)
  matrix products  75.7 us (25%)
  local copies, waits for them, and re-layouts  26.1 us (9%)
  between operations  14.5 us (5%)
  other arithmetic  7.68 us (3%)
    reduce_scatter x1, waiting for transfers between devices, per_device(): lax.psum_scatter(author_part.reshape(col_blocks * side, width), 'prow', s...  74.7 us
    all_gather x1, waiting for transfers between devices, per_device(): authors = lax.all_gather(author_x, 'prow', axis=0, tiled=True)  43.8 us
    reduce_scatter x1, waiting for transfers between devices, per_device(): lax.psum_scatter(partial_value, 'pcol', scatter_dimension=0, tiled=True)  36.3 us
    dot_general x2, matrix products, second_hop(): jnp.einsum('kc,kaf->caf', placing, product, precision=lax.Precision.HIGHEST)  22.4 us
    dot_general x2, matrix products, first_hop(): jnp.einsum('kr,kpf->rpf', placing, product, precision=lax.Precision.HIGHEST)  22.3 us
    all_gather x1, waiting for transfers between devices, per_device(): lax.all_gather(outgoing, 'pcol', axis=0, tiled=True)  19.5 us
    dot_general x2, matrix products, second_hop(): jnp.einsum('kpa,kpf->kaf', content_now, picked, preferred_element_type=jn...  11.1 us
    dot_general x2, matrix products, first_hop(): jnp.einsum('kpa,kaf->kpf', content_now, picked, preferred_element_type=jn...  11 us
  transfers between devices with their start and end apart: 4, of which 4 were waited for; matrix products, arithmetic and copies ran while one was open for 2% of the time, Pallas kernels for 0%

commit v1 on v0

--- a/solution.py
+++ b/solution.py
@@ -2,6 +2,7 @@
 import jax.numpy as jnp
 from jax import lax
 from jax.sharding import PartitionSpec as P
+from jax.lax import all_to_all, psum
 
 GROUP = 16
 
@@ -34,7 +35,13 @@
     )
     contents = block_vals.reshape(groups, GROUP, side, side)
     self_term = jnp.dot(paper_x, w_self, preferred_element_type=jnp.float32)
-    authors = lax.all_gather(author_x, "prow", axis=0, tiled=True)
+    tmp = all_to_all(
+        jnp.stack(tuple((author_x for _ in range(psum(1, "prow")))), axis=0),
+        axis_name="prow",
+        split_axis=0,
+        concat_axis=0,
+    )
+    authors = jnp.concatenate(tmp, axis=0)
     messages = jnp.stack(
         [
             jnp.dot(authors, w_rel[index], preferred_element_type=jnp.float32)

time: 300 us -> 297 us (0.990)
  waiting for transfers between devices: 175 us -> 165 us
  starting transfers between devices: 0.34 us -> 7.61 us
    all_gather x1 -> x0, waiting for transfers between devices: 43.8 us -> none  [per_device(): authors = lax.all_gather(author_x, 'prow', axis=0, tiled=True)]
    all_to_all x0 -> x1, waiting for transfers between devices: none -> 33.5 us  [per_device(): all_to_all(jnp.stack(tuple((author_x for _ in range(psum(1, 'prow')))), a...]
    all_to_all x0 -> x1, starting transfers between devices: none -> 7.31 us  [per_device(): all_to_all(jnp.stack(tuple((author_x for _ in range(psum(1, 'prow')))), a...]
  transfers between devices with their start and end apart: 4 -> 4, of which waited for: 4 -> 4; matrix products, arithmetic and copies ran while one was open for 2% -> 1% of each run, Pallas kernels for 0% -> 0%
where the time goes in v1:
time: 297 us; the launch traced here: 296 us
  waiting for transfers between devices  165 us (56%)
  matrix products  75.3 us (25%)
  local copies, waits for them, and re-layouts  28.4 us (10%)
  between operations  14.5 us (5%)
  starting transfers between devices  7.61 us (3%)
  other arithmetic  5.73 us (2%)
    reduce_scatter x1, waiting for transfers between devices, per_device(): lax.psum_scatter(author_part.reshape(col_blocks * side, width), 'prow', s...  74.5 us
    reduce_scatter x1, waiting for transfers between devices, per_device(): lax.psum_scatter(partial_value, 'pcol', scatter_dimension=0, tiled=True)  37 us
    all_to_all x1, waiting for transfers between devices, per_device(): all_to_all(jnp.stack(tuple((author_x for _ in range(psum(1, 'prow')))), a...  33.5 us
    dot_general x2, matrix products, second_hop(): jnp.einsum('kc,kaf->caf', placing, product, precision=lax.Precision.HIGHEST)  22.4 us
    dot_general x2, matrix products, first_hop(): jnp.einsum('kr,kpf->rpf', placing, product, precision=lax.Precision.HIGHEST)  22.3 us
    all_gather x1, waiting for transfers between devices, per_device(): lax.all_gather(outgoing, 'pcol', axis=0, tiled=True)  19.5 us
    dot_general x2, matrix products, second_hop(): jnp.einsum('kpa,kpf->kaf', content_now, picked, preferred_element_type=jn...  11.2 us
    dot_general x2, matrix products, first_hop(): jnp.einsum('kpa,kaf->kpf', content_now, picked, preferred_element_type=jn...  11 us
  transfers between devices with their start and end apart: 4, of which 4 were waited for; matrix products, arithmetic and copies ran while one was open for 1% of the time, Pallas kernels for 0%

profile of v1, /device:TPU:0, one launch (start us, length us, event | category | flops | bytes accessed | tf_op | source)
XLA Modules:
  0.0 296.3 jit_solution(11222777386300679066)
XLA Ops:
  7.2 2.3 stack.11
  9.5 7.3 %all-to-all-start = ((bf16[8,128,768]{2,1,0:T(8,128)(2,1)}), bf16[8,128,768]{2,1,0:T(8,128)(2,1)S(1)}, u32[]{:S(2)}, u32[]{:S(2)}) async-start(bf16[8,128,768]{2,1,0:T(8,128)(2,1)} %stack.11), calls=%async_computation | async-start | bytes 3145728 | tf_op jit(solution)/shard_map/all_to_all | solution.py:38
  16.8 0.5 broadcast.118
  17.4 0.7 reduce.9
  18.1 0.7 reduce.11
  18.9 0.7 reduce.10
  20.3 33.5 %all-to-all-done = bf16[8,128,768]{2,1,0:T(8,128)(2,1)S(1)} async-done(((bf16[8,128,768]{2,1,0:T(8,128)(2,1)}), bf16[8,128,768]{2,1,0:T(8,128)(2,1)S(1)}, u32[]{:S(2)}, u32[]{:S(2)}) %all-to-all-start) | async-done | bytes 1572896 | tf_op jit(solution)/shard_map/all_to_all | solution.py:38
  53.8 2.8 fusion.41
  56.6 1.4 fusion.42
  58.0 2.0 pad_maximum_fusion
  60.0 42.0 %while.22 = (s32[]{:T(128)}, f32[8,128,768]{2,0,1:T(8,128)}, s32[2,16]{1,0:T(2,128)S(1)}, f32[2,16]{1,0:T(2,128)S(1)}, bf16[2,16,128,128]{3,2,1,0:T(8,128)(2,1)S...) while((s32[]{:T(128)}, f32[8,128,768]{2,0,1:T(8,128)}, ...), condition=%wide.region_1.2_spmd.clone, body=%wide.region_0.1_spmd.clone.sunk | while | flops 555222400 | bytes 28840768 | solution.py:70
  60.0 4.3 %gather_fusion = bf16[16,128,768]{2,1,0:T(8,128)(2,1)} fusion(bf16[16,128,768]{2,1,0:T(8,128)(2,1)} %get-tuple-element.297, s32[1024]{0:T(1024)S(1)} %pad_clamp_fusion.4), kind=kCustom, calls=%fused_computation.clone.clone.1 | custom fusion | bytes 6291520 | tf_op jit(solution)/shard_map/while/body/eval_jaxpr/gather | solution.py:59
  64.3 5.5 %fusion.78 = f32[16,128,768]{2,1,0:T(8,128)} fusion(bf16[16,128,768]{2,1,0:T(8,128)(2,1)} %gather_fusion, bf16[2,16,128,128]{3,2,1,0:T(8,128)(2,1)S(1)} %get-tuple-element.294, s32[]{:T(128)} %get-tuple-element.280), kind=kOutput, calls=%fused_computation.7.clone.1 | convolution fusion | flops 402653184 | bytes 9961476 | tf_op jit(solution)/shard_map/while/body/eval_jaxpr/kpa,kaf->kpf/dot_general | solution.py:60
  69.9 10.9 %select_add_fusion.4 = f32[8,128,768]{2,0,1:T(8,128)} fusion(f32[8,128,768]{2,0,1:T(8,128)} %get-tuple-element.281, f32[16,128,768]{2,1,0:T(8,128)} %fusion.78, pred[]{:T(512)S(6)} %compare.6, f32[16]{0:T(128)S(1)} %fusion.79, s32[16]{0:T(128)S(1)} %fusion.80), kind=kOutput, calls=%fused_computation.6.clone.1 | convolution fusion | flops 152568064 | bytes 12583041 | tf_op jit(solution)/shard_map/while/body/eval_jaxpr/kr,kpf->rpf/dot_general | solution.py:65
  80.8 4.3 %gather_fusion = bf16[16,128,768]{2,1,0:T(8,128)(2,1)} fusion(bf16[16,128,768]{2,1,0:T(8,128)(2,1)} %get-tuple-element.297, s32[1024]{0:T(1024)S(1)} %pad_clamp_fusion.4), kind=kCustom, calls=%fused_computation.clone.clone.1 | custom fusion | bytes 6291520 | tf_op jit(solution)/shard_map/while/body/eval_jaxpr/gather | solution.py:59
  85.1 5.5 %fusion.78 = f32[16,128,768]{2,1,0:T(8,128)} fusion(bf16[16,128,768]{2,1,0:T(8,128)(2,1)} %gather_fusion, bf16[2,16,128,128]{3,2,1,0:T(8,128)(2,1)S(1)} %get-tuple-element.294, s32[]{:T(128)} %get-tuple-element.280), kind=kOutput, calls=%fused_computation.7.clone.1 | convolution fusion | flops 402653184 | bytes 9961476 | tf_op jit(solution)/shard_map/while/body/eval_jaxpr/kpa,kaf->kpf/dot_general | solution.py:60
  90.6 11.4 %select_add_fusion.4 = f32[8,128,768]{2,0,1:T(8,128)} fusion(f32[8,128,768]{2,0,1:T(8,128)} %get-tuple-element.281, f32[16,128,768]{2,1,0:T(8,128)} %fusion.78, pred[]{:T(512)S(6)} %compare.6, f32[16]{0:T(128)S(1)} %fusion.79, s32[16]{0:T(128)S(1)} %fusion.80), kind=kOutput, calls=%fused_computation.6.clone.1 | convolution fusion | flops 152568064 | bytes 12583041 | tf_op jit(solution)/shard_map/while/body/eval_jaxpr/kr,kpf->rpf/dot_general | solution.py:65
  102.0 4.6 %copy.12 = f32[8,128,768]{2,1,0:T(8,128)} copy(f32[8,128,768]{2,0,1:T(8,128)} %get-tuple-element.91) | data formatting | bytes 6291456 | tf_op jit(solution)/shard_map/while | solution.py:70
  106.6 37.0 %reduce-scatter.3.cloned.1.call-done = f32[256,768]{1,0:T(8,128)} async-done(((f32[1024,768]{1,0:T(8,128)}), f32[256,768]{1,0:T(8,128)}) %reduce-scatter.3.cloned.1.call-update) | async-done | bytes 786448 | tf_op jit(solution)/shard_map/reduce_scatter | solution.py:72
  143.7 1.6 fusion.44
  145.3 2.6 convolution_convert_fusion.2
  148.2 19.5 %all-gather.2.cloned.1.call-done = bf16[1024,768]{1,0:T(8,128)(2,1)} async-done(((bf16[256,768]{1,0:T(8,128)(2,1)}), bf16[1024,768]{1,0:T(8,128)(2,1)}) %all-gather.2.cloned.1.call-update) | async-done | bytes 1572880 | tf_op jit(solution)/shard_map/all_gather | solution.py:75
  167.8 41.3 %while.23 = (s32[]{:T(128)}, f32[8,128,768]{2,0,1:T(8,128)}, s32[2,16]{1,0:T(2,128)S(1)}, f32[2,16]{1,0:T(2,128)S(1)}, bf16[2,16,128,128]{3,2,1,0:T(8,128)(2,1)S...) while((s32[]{:T(128)}, f32[8,128,768]{2,0,1:T(8,128)}, ...), condition=%wide.region_4.5_spmd.clone, body=%wide.region_3.4_spmd.clone.sunk | while | flops 555222336 | bytes 28840696 | solution.py:92
  167.8 3.8 %gather_fusion.1 = bf16[16,128,768]{2,1,0:T(8,128)(2,1)} fusion(bf16[8,128,768]{2,1,0:T(8,128)(2,1)} %get-tuple-element.324, s32[1024]{0:T(1024)S(1)} %pad_clamp_fusion.5), kind=kCustom, calls=%fused_computation.1.clone.clone.1 | custom fusion | bytes 6291520 | tf_op jit(solution)/shard_map/while/body/eval_jaxpr/gather | solution.py:81
  171.6 5.6 %fusion.86 = f32[16,128,768]{2,1,0:T(8,128)} fusion(bf16[16,128,768]{2,1,0:T(8,128)(2,1)} %gather_fusion.1, bf16[2,16,128,128]{3,2,1,0:T(8,128)(2,1)S(1)} %get-tuple-element.322, s32[]{:T(128)} %get-tuple-element.309), kind=kOutput, calls=%fused_computation.32.clone.1 | convolution fusion | flops 402653184 | bytes 9961476 | tf_op jit(solution)/shard_map/while/body/eval_jaxpr/kpa,kpf->kaf/dot_general | solution.py:82
  177.2 11.0 %select_add_fusion.5 = f32[8,128,768]{2,0,1:T(8,128)} fusion(f32[8,128,768]{2,0,1:T(8,128)} %get-tuple-element.310, f32[16,128,768]{2,1,0:T(8,128)} %fusion.86, pred[]{:T(512)S(6)} %compare.7, f32[16]{0:T(128)S(1)} %fusion.87, s32[16]{0:T(128)S(1)} %fusion.88), kind=kOutput, calls=%fused_computation.31.clone.1 | convolution fusion | flops 152568064 | bytes 12583041 | tf_op jit(solution)/shard_map/while/body/eval_jaxpr/kc,kaf->caf/dot_general | solution.py:87
  188.2 3.8 %gather_fusion.1 = bf16[16,128,768]{2,1,0:T(8,128)(2,1)} fusion(bf16[8,128,768]{2,1,0:T(8,128)(2,1)} %get-tuple-element.324, s32[1024]{0:T(1024)S(1)} %pad_clamp_fusion.5), kind=kCustom, calls=%fused_computation.1.clone.clone.1 | custom fusion | bytes 6291520 | tf_op jit(solution)/shard_map/while/body/eval_jaxpr/gather | solution.py:81
  192.0 5.6 %fusion.86 = f32[16,128,768]{2,1,0:T(8,128)} fusion(bf16[16,128,768]{2,1,0:T(8,128)(2,1)} %gather_fusion.1, bf16[2,16,128,128]{3,2,1,0:T(8,128)(2,1)S(1)} %get-tuple-element.322, s32[]{:T(128)} %get-tuple-element.309), kind=kOutput, calls=%fused_computation.32.clone.1 | convolution fusion | flops 402653184 | bytes 9961476 | tf_op jit(solution)/shard_map/while/body/eval_jaxpr/kpa,kpf->kaf/dot_general | solution.py:82
  197.6 11.4 %select_add_fusion.5 = f32[8,128,768]{2,0,1:T(8,128)} fusion(f32[8,128,768]{2,0,1:T(8,128)} %get-tuple-element.310, f32[16,128,768]{2,1,0:T(8,128)} %fusion.86, pred[]{:T(512)S(6)} %compare.7, f32[16]{0:T(128)S(1)} %fusion.87, s32[16]{0:T(128)S(1)} %fusion.88), kind=kOutput, calls=%fused_computation.31.clone.1 | convolution fusion | flops 152568064 | bytes 12583041 | tf_op jit(solution)/shard_map/while/body/eval_jaxpr/kc,kaf->caf/dot_general | solution.py:87
  209.0 4.6 %copy.13 = f32[8,128,768]{2,1,0:T(8,128)} copy(f32[8,128,768]{2,0,1:T(8,128)} %get-tuple-element.92) | data formatting | bytes 6291456 | tf_op jit(solution)/shard_map/while | solution.py:92
  213.6 74.5 %reduce-scatter.5.cloned.1.call-done = f32[128,768]{1,0:T(8,128)} async-done(((f32[1024,768]{1,0:T(8,128)}), f32[128,768]{1,0:T(8,128)}) %reduce-scatter.5.cloned.1.call-update) | async-done | bytes 393232 | tf_op jit(solution)/shard_map/reduce_scatter | solution.py:93
  288.1 1.7 convert_element_type.24
  (44 shorter events, 0.8 us)
Async XLA Ops:
  7.2 136.5 %copy-start = (bf16[768,768]{1,0:T(8,128)(2,1)S(1)}, bf16[768,768]{1,0:T(8,128)(2,1)}, u32[]{:S(2)}) copy-start(bf16[768,768]{1,0:T(8,128)(2,1)} %param.16) | copy-start | bytes 3538948
  7.2 10.2 %copy-start.5 = (s32[1,1,32]{2,1,0:T(1,128)S(1)}, s32[1,1,32]{2,1,0:T(1,128)}, u32[]{:S(2)}) copy-start(s32[1,1,32]{2,1,0:T(1,128)} %param.19) | copy-start | bytes 388
  7.2 10.9 %copy-start.6 = (s32[1,1,32]{2,1,0:T(1,128)S(1)}, s32[1,1,32]{2,1,0:T(1,128)}, u32[]{:S(2)}) copy-start(s32[1,1,32]{2,1,0:T(1,128)} %param.20) | copy-start | bytes 388
  7.2 11.7 %copy-start.7 = (s32[1,1,32]{2,1,0:T(1,128)S(1)}, s32[1,1,32]{2,1,0:T(1,128)}, u32[]{:S(2)}) copy-start(s32[1,1,32]{2,1,0:T(1,128)} %param.21) | copy-start | bytes 388
  9.5 44.3 %all-to-all-start = ((bf16[8,128,768]{2,1,0:T(8,128)(2,1)}), bf16[8,128,768]{2,1,0:T(8,128)(2,1)S(1)}, u32[]{:S(2)}, u32[]{:S(2)}) async-start(bf16[8,128,768]{2,1,0:T(8,128)(2,1)} %stack.11), calls=%async_computation | async-start | bytes 3145728 | tf_op jit(solution)/shard_map/all_to_all | solution.py:38
  16.8 126.9 %reduce-scatter.3.cloned.1.call-start = ((), (), s32[]{:S(2)}) async-start(), calls=%async_computation.3 | async-start | bytes 3932160 | tf_op jit(solution)/shard_map/reduce_scatter | solution.py:72
  53.8 2.8 copy-start.4
  58.0 2.0 copy-start.1
  106.6 37.1 %copy-start.3 = (bf16[256,768]{1,0:T(8,128)(2,1)S(1)}, bf16[256,768]{1,0:T(8,128)(2,1)}, u32[]{:S(2)}) copy-start(bf16[256,768]{1,0:T(8,128)(2,1)} %param.14) | copy-start | bytes 1179652
  106.6 61.2 %all-gather.2.cloned.1.call-start = ((), (), s32[]{:S(2)}) async-start(), calls=%async_computation.4 | async-start | bytes 1966080 | tf_op jit(solution)/shard_map/all_gather | solution.py:75
  145.3 22.5 %copy-start.2 = (bf16[256,768]{1,0:T(8,128)(2,1)}, bf16[256,768]{1,0:T(8,128)(2,1)S(1)}, u32[]{:S(2)}) copy-start(bf16[256,768]{1,0:T(8,128)(2,1)S(1)} %fusion.44) | copy-start | bytes 1179652
  148.0 140.1 %reduce-scatter.5.cloned.1.call-start = ((), (), s32[]{:S(2)}) async-start(), calls=%async_computation.5 | async-start | bytes 3538944 | tf_op jit(solution)/shard_map/reduce_scatter | solution.py:93
Sparse Core Ops, SparseCore 0:
  106.7 36.9 reduce-scatter.2
  148.1 19.6 all-gather.1
  213.7 74.3 reduce-scatter.4
